TPU v7x, 128 devices: a whole 4x4x4 slice. The times are simulated.
128 devices in a mesh: bin: 4 (over y), grp: 32 (over x, z, core).
Axes of the slice: x: 4, y: 4, z: 4, core: 2. Of those that a mesh axis runs over, the one named last changes fastest.
Arguments:
- templates: bfloat16 [131072, 512], P(('bin', 'grp')), may hold values from -6 to 6
- owner_device: int32 [131072, 1], P(('bin', 'grp')), may hold values from 0 to 127; in each aligned block of 1024 rows (0 to 1023, 1024 to 2047, ...) at most 16 rows name the same one
- rate_code: int32 [131072], P(('bin', 'grp')), may hold values from 0 to 4
- rate_gains: float32 [5, 512], replicated, may hold values from 0.5 to 2
- sketch: float32 [512, 256], replicated, may hold values from -6 to 6
- strain: float32 [2, 262144], P(None, 'grp'), may hold values from -6 to 6
Outputs:
- mixing: bfloat16 [131072, 256], P(('bin', 'grp'))
- spectrum: float32 [4, 256], P('bin')
- filtered_0: bfloat16 [4, 2, 262144, 256], P('bin', None, 'grp')
- filtered_1: bfloat16 [4, 2, 131072, 256], P('bin', None, 'grp')
- filtered_2: bfloat16 [4, 2, 65536, 256], P('bin', None, 'grp')
- filtered_3: bfloat16 [4, 2, 32768, 256], P('bin', None, 'grp')
- filtered_4: bfloat16 [4, 2, 16384, 256], P('bin', None, 'grp')
Inputs may be any that keep to these rules, and one draw needn't show every extreme that they name: `owner_device`: among the rows of one device, no device is named by more than 16 rows, and some device is named by exactly 16 rows.
All inputs are finite; a program needn't handle non-finite values.
Results may differ from a plain program's by a relative error of at most 0.0059.
Values may be sent and summed in bfloat16 or wider, within the bound.
A program may use at most 128 MiB of HBM per device.

v0:
```python
import math
import jax
import jax.numpy as jnp
from jax import lax
from jax.sharding import PartitionSpec as P

highest = lax.Precision.HIGHEST
inv_root_two = 0.7071067811865476


def shifted(x, axis, by):
    length = lax.axis_size(axis)
    pairs = [(i, i + by) for i in range(length) if 0 <= i + by < length]
    return lax.ppermute(x, axis, pairs)


def whiten_rows(templates, rate_code, rate_gains):
    factor = jnp.zeros(templates.shape, jnp.float32)
    for rate_level in range(rate_gains.shape[0]):
        factor = factor + jnp.where(
            (rate_code == rate_level)[:, None], rate_gains[rate_level][None, :], jnp.float32(0.0)
        )
    return (templates.astype(jnp.float32) * factor).astype(jnp.bfloat16)


def strain_levels(strain, count):
    current = strain
    level_list = []
    for rate_level in range(count):
        if rate_level > 0:
            paired = current.reshape(current.shape[0], -1, 2)
            current = (paired[:, :, 0] + paired[:, :, 1]) * inv_root_two
        level_list.append(current.astype(jnp.bfloat16))
    return level_list


def filter_level(history, rounded, basis_bf, stride):
    tap_rows = basis_bf[::stride]
    joined = jnp.concatenate([history[:, 1:], rounded], axis=1)
    return lax.conv_general_dilated(
        joined[:, :, None],
        tap_rows[::-1][:, None, :],
        (1,),
        "VALID",
        dimension_numbers=("NWC", "WIO", "NWC"),
        preferred_element_type=jnp.float32,
    )


def basis_from(product):
    inner_gram = jnp.dot(product.T, product, precision=highest)
    lower_factor = jnp.linalg.cholesky(inner_gram)
    basis_bf = jax.scipy.linalg.solve_triangular(lower_factor, product.T, lower=True).T.astype(
        jnp.bfloat16
    )
    return (basis_bf, jnp.diagonal(lower_factor))


def local(templates, owner_device, rate_code, rate_gains, sketch, strain):
    tpl_rows = templates.shape[0]
    slice_len = templates.shape[1]
    group_size = lax.axis_size("grp")
    bin_count = lax.axis_size("bin")
    devices = bin_count * group_size
    capacity = 2 * tpl_rows // devices
    scale_down = tpl_rows * group_size * math.sqrt(slice_len)
    whitened = whiten_rows(templates, rate_code, rate_gains)
    target = owner_device[:, 0]
    member_table = (target[:, None] == jnp.arange(devices, dtype=jnp.int32)[None, :]).astype(
        jnp.int32
    )
    rank_in_dest = jnp.sum(jnp.cumsum(member_table, axis=0) * member_table, axis=1) - 1
    slot_index = target * capacity + rank_in_dest
    outgoing = jnp.zeros((devices * capacity, slice_len), jnp.bfloat16).at[slot_index].set(whitened)
    received = lax.all_to_all(outgoing, ("bin", "grp"), split_axis=0, concat_axis=0, tiled=True)
    partial_gram = lax.dot_general(
        received, received, (((0,), (0,)), ((), ())), preferred_element_type=jnp.float32
    )
    gram_total = lax.psum(partial_gram, "grp")
    product = jnp.dot(gram_total, sketch, precision=highest)
    basis_bf, diag_here = basis_from(product)
    coeffs = jnp.dot(received, basis_bf, preferred_element_type=jnp.float32).astype(jnp.bfloat16)
    returned = lax.all_to_all(coeffs, ("bin", "grp"), split_axis=0, concat_axis=0, tiled=True)
    mixing = returned[slot_index]
    spectrum = (diag_here / scale_down)[None, :]
    levels = strain_levels(strain, rate_gains.shape[0])
    rim_list = [
        levels[rate_level][:, -(slice_len >> rate_level) :] for rate_level in range(len(levels))
    ]
    history = shifted((rim_list[0], rim_list[1], rim_list[2], rim_list[3], rim_list[4]), "grp", 1)
    filtered = []
    for rate_level in range(len(levels)):
        result_level = filter_level(
            history[rate_level], levels[rate_level], basis_bf, 2**rate_level
        )
        filtered.append(result_level.astype(jnp.bfloat16)[None])
    return (mixing, spectrum, filtered[0], filtered[1], filtered[2], filtered[3], filtered[4])


def solution(mesh):
    return jax.shard_map(
        local,
        mesh=mesh,
        in_specs=(
            P(("bin", "grp"), None),
            P(("bin", "grp"), None),
            P(("bin", "grp")),
            P(),
            P(),
            P(None, "grp"),
        ),
        out_specs=(
            P(("bin", "grp"), None),
            P("bin", None),
            P("bin", None, "grp", None),
            P("bin", None, "grp", None),
            P("bin", None, "grp", None),
            P("bin", None, "grp", None),
            P("bin", None, "grp", None),
        ),
        check_vma=False,
    )
```

profile of v0, /device:TPU:1, one launch (start us, length us, event | category | flops | bytes accessed | tf_op | source)
XLA Modules:
  0.0 488.1 jit_solution(5350892277837483940)
XLA Ops:
  9.0 7.3 %scatter_custom_fusion = bf16[2048,512]{1,0:T(8,128)(2,1)} fusion(s32[1024]{0:T(1024)S(1)} %bitcast.143, bf16[1024,512]{1,0:T(8,128)(2,1)S(1)} %copy-done.3, f32[512]{0:T(512)S(1)} %bitcast.149, f32[512]{0:T(512)S(1)} %bitcast.150, f32[512]{0:T(512)S(1)} %bitcast.147, f32[512]{0:T(512)S(1)} %bitcast.148, f32[]{:T(128)} %constant.105.clone.1, ...), kind=kCustom, calls=%fused_computation.26 | custom fusion | flops 6291456 | bytes 3161094 | tf_op jit(solution)/shard_map/scatter | solution.py:74
  16.3 12.0 %all-to-all-start = ((bf16[128,16,512]{2,1,0:T(8,128)(2,1)}), bf16[128,16,512]{2,1,0:T(8,128)(2,1)}, u32[]{:S(2)}, u32[]{:S(2)}) async-start(bf16[128,16,512]{2,1,0:T(8,128)(2,1)} %bitcast.12), calls=%async_computation | async-start | bytes 4194304 | tf_op jit(solution)/shard_map/all_to_all | solution.py:75
  28.4 3.7 collective-permute-start
  32.1 6.4 %reshape.114 = f32[2,4096,2]{2,1,0:T(8,128)} reshape(f32[2,8192]{1,0:T(2,128)S(1)} %copy-done.6) | data formatting | bytes 131072 | tf_op jit(solution)/shard_map/reshape | solution.py:31
  38.5 5.9 %convert_reduce_fusion = bf16[2,4096]{1,0:T(2,128)(2,1)S(1)} fusion(f32[2,4096,2]{2,1,0:T(8,128)} %reshape.114), kind=kLoop, calls=%fused_computation.17 | loop fusion | flops 24576 | bytes 81920 | tf_op jit(solution)/shard_map/convert_element_type | solution.py:33
  52.4 3.6 collective-permute-start.2
  71.7 4.5 convolution_bitcast_fusion
  78.0 104.7 %all-reduce.3.cloned.1.call-done = f32[512,512]{1,0:T(8,128)} async-done(((f32[512,512]{1,0:T(8,128)}), f32[512,512]{1,0:T(8,128)}) %all-reduce.3.cloned.1.call-update) | async-done | bytes 1048592 | tf_op jit(solution)/shard_map/psum | solution.py:79
  186.2 11.7 %cholesky.50 = f32[128,128]{1,0:T(8,128)S(1)} custom-call(f32[128,128]{1,0:T(8,128)S(1)} %cholesky.118), custom_call_target="Cholesky" | custom-call | tf_op jit(solution)/shard_map/jit(cholesky)/cholesky | solution.py:52
  197.9 9.8 %custom-call.15 = f32[1,128,128]{1,2,0:T(8,128)S(1)} custom-call(f32[1,128,128]{2,1,0:T(8,128)S(1)} %get-tuple-element.30), custom_call_target="InvertDiagBlocksLowerTriangular" | custom-call | tf_op jit(solution)/shard_map/jit(cholesky)/cholesky | solution.py:52
  208.2 12.2 %cholesky.105 = f32[128,128]{1,0:T(8,128)S(1)} custom-call(f32[128,128]{1,0:T(8,128)S(1)} %convolution_subtract_fusion.1), custom_call_target="Cholesky" | custom-call | tf_op jit(solution)/shard_map/jit(cholesky)/cholesky | solution.py:52
  222.5 4.0 while.1
  226.5 19.7 %custom-call.16 = f32[2,128,128]{1,2,0:T(8,128)S(1)} custom-call(f32[2,128,128]{2,1,0:T(8,128)S(1)} %get-tuple-element.14), custom_call_target="InvertDiagBlocksLowerTriangular" | custom-call | tf_op jit(solution)/shard_map/jit(_solve_triangular)/triangular_solve | solution.py:53
  248.5 6.6 %slice.147 = bf16[256,256]{0,1:T(8,128)(2,1)} slice(bf16[512,256]{0,1:T(8,128)(2,1)S(1)} %fusion.31), slice={[0:512:2], [0:256:1]} | slice | bytes 262144 | tf_op jit(solution)/shard_map/slice | solution.py:38
  261.3 3.3 convolution_convert_fusion
  264.6 8.5 %all-to-all-start.1 = ((bf16[128,16,256]{2,1,0:T(8,128)(2,1)}), bf16[128,16,256]{2,1,0:T(8,128)(2,1)}, u32[]{:S(2)}, u32[]{:S(2)}) async-start(bf16[128,16,256]{2,1,0:T(8,128)(2,1)} %bitcast.21), calls=%async_computation.1 | async-start | bytes 2097152 | tf_op jit(solution)/shard_map/all_to_all | solution.py:83
  276.4 123.6 %select_convert_fusion = bf16[16,1088,256]{2,0,1:T(8,128)(2,1)} fusion(pred[16,1088]{0,1:T(8,128)(4,1)S(1)} %bitcast.152, bf16[16,1599,1]{0,2,1:T(2,128)(2,1)S(1)} %copy.25, bf16[512,1,256]{2,1,0:T(2,128)(2,1)S(1)} %copy.26), kind=kOutput, calls=%fused_computation.5 | convolution fusion | flops 4572315648 | bytes 9243616 | tf_op jit(solution)/shard_map/conv_general_dilated | solution.py:40
  400.1 10.2 %copy.27 = bf16[16,1088,256]{2,1,0:T(8,128)(2,1)} copy(bf16[16,1088,256]{2,0,1:T(8,128)(2,1)} %select_convert_fusion) | data formatting | bytes 17825792 | tf_op jit(solution)/shard_map/convert_element_type | solution.py:96
  410.3 7.4 %slice_bitcast_fusion = bf16[1,2,8192,256]{3,2,1,0:T(8,128)(2,1)} fusion(bf16[2,8704,256]{2,1,0:T(8,128)(2,1)} %bitcast.129), kind=kLoop, calls=%fused_computation.7 | loop fusion | bytes 16777216 | tf_op jit(solution)/shard_map/broadcast_in_dim | solution.py:96
  418.3 31.3 %select_convert_fusion.1 = bf16[16,544,256]{2,0,1:T(8,128)(2,1)S(1)} fusion(pred[16,544]{0,1:T(8,128)(4,1)S(1)} %bitcast.153, bf16[16,799,1]{0,2,1:T(2,128)(2,1)S(1)} %copy-done.5, bf16[256,1,256]{2,1,0:T(2,128)(2,1)S(1)} %copy.29), kind=kOutput, calls=%fused_computation.6 | convolution fusion | flops 1145307136 | bytes 4621792 | tf_op jit(solution)/shard_map/conv_general_dilated | solution.py:40
  449.6 3.6 copy.30
  453.6 8.4 %select_convert_fusion.2 = bf16[16,272,256]{2,0,1:T(8,128)(2,1)S(1)} fusion(pred[16,272]{0,1:T(8,128)(4,1)S(1)} %copy-done.19, bf16[16,399,1]{0,2,1:T(2,128)(2,1)S(1)} %copy-done.10, bf16[128,1,256]{2,1,0:T(2,128)(2,1)S(1)} %copy.32), kind=kOutput, calls=%fused_computation.8 | convolution fusion | flops 287440896 | bytes 2310880 | tf_op jit(solution)/shard_map/conv_general_dilated | solution.py:40
  470.6 4.5 slice_bitcast_fusion.1
  475.0 6.0 %gather_fusion = bf16[1024,256]{1,0:T(8,128)(2,1)} fusion(bf16[2048,256]{1,0:T(8,128)(2,1)} %bitcast.22, s32[1024]{0:T(1024)S(1)} %copy-done.14), kind=kCustom, calls=%fused_computation | custom fusion | bytes 1052672 | tf_op jit(solution)/shard_map/gather | solution.py:84
  (169 shorter events, 57.0 us)
Async XLA Ops:
  7.2 175.5 %copy-start = (f32[512,256]{1,0:T(8,128)S(1)}, f32[512,256]{1,0:T(8,128)}, u32[]{:S(2)}) copy-start(f32[512,256]{1,0:T(8,128)} %param.10) | copy-start | bytes 1572868
  7.2 1.8 copy-start.16
  7.2 1.8 copy-start.3
  16.3 12.0 %copy-start.6 = (f32[2,8192]{1,0:T(2,128)S(1)}, f32[2,8192]{1,0:T(2,128)}, u32[]{:S(2)}) copy-start(f32[2,8192]{1,0:T(2,128)} %param.11) | copy-start | bytes 196612
  16.3 55.3 %all-to-all-start = ((bf16[128,16,512]{2,1,0:T(8,128)(2,1)}), bf16[128,16,512]{2,1,0:T(8,128)(2,1)}, u32[]{:S(2)}, u32[]{:S(2)}) async-start(bf16[128,16,512]{2,1,0:T(8,128)(2,1)} %bitcast.12), calls=%async_computation | async-start | bytes 4194304 | tf_op jit(solution)/shard_map/all_to_all | solution.py:75
  28.3 154.4 %all-reduce.3.cloned.1.call-start = ((), (), s32[]{:S(2)}) async-start(), calls=%async_computation.2 | async-start | bytes 2097152 | tf_op jit(solution)/shard_map/psum | solution.py:79
  28.4 43.2 %collective-permute-start = (bf16[2,512]{1,0:T(2,128)(2,1)S(1)}, bf16[2,512]{1,0:T(2,128)(2,1)S(1)}, u32[]{:S(2)}, u32[]{:S(2)}) collective-permute-start(bf16[2,512]{1,0:T(2,128)(2,1)S(1)} %slice.190), channel_id=1, source_target_pairs={{0,1},{1,2},{2,3},{3,4},{4,5},{5,6},{6,7},{7,8},{8,9},{9,10},{10,1... | collective-permute-start | bytes 6152 | tf_op jit(solution)/shard_map/ppermute | solution.py:14
  38.5 8.1 %copy-start.2 = (f32[2,4096,2]{2,1,0:T(8,128)S(1)}, f32[2,4096,2]{2,1,0:T(8,128)}, u32[]{:S(2)}) copy-start(f32[2,4096,2]{2,1,0:T(8,128)} %reshape.114) | copy-start | bytes 196612
  44.4 25.7 %collective-permute-start.1 = (bf16[2,256]{1,0:T(2,128)(2,1)S(1)}, bf16[2,256]{1,0:T(2,128)(2,1)S(1)}, u32[]{:S(2)}, u32[]{:S(2)}) collective-permute-start(bf16[2,256]{1,0:T(2,128)(2,1)S(1)} %slice.196), channel_id=1, source_target_pairs={{0,1},{1,2},{2,3},{3,4},{4,5},{5,6},{6,7},{7,8},{8,9},{9,10},{10,1... | collective-permute-start | bytes 3080 | tf_op jit(solution)/shard_map/ppermute | solution.py:14
  52.4 16.5 %collective-permute-start.2 = (bf16[2,128]{1,0:T(2,128)(2,1)S(1)}, bf16[2,128]{1,0:T(2,128)(2,1)S(1)}, u32[]{:S(2)}, u32[]{:S(2)}) collective-permute-start(bf16[2,128]{1,0:T(2,128)(2,1)S(1)} %slice.202), channel_id=1, source_target_pairs={{0,1},{1,2},{2,3},{3,4},{4,5},{5,6},{6,7},{7,8},{8,9},{9,10},{10,1... | collective-permute-start | bytes 1544 | tf_op jit(solution)/shard_map/ppermute | solution.py:14
  59.0 8.8 %collective-permute-start.3 = (bf16[2,64]{1,0:T(2,128)(2,1)S(1)}, bf16[2,64]{1,0:T(2,128)(2,1)S(1)}, u32[]{:S(2)}, u32[]{:S(2)}) collective-permute-start(bf16[2,64]{1,0:T(2,128)(2,1)S(1)} %slice.207), channel_id=1, source_target_pairs={{0,1},{1,2},{2,3},{3,4},{4,5},{5,6},{6,7},{7,8},{8,9},{9,10},{10,1... | collective-permute-start | bytes 776 | tf_op jit(solution)/shard_map/ppermute | solution.py:14
  62.7 4.0 collective-permute-start.4
  264.6 11.8 %copy-start.17 = (pred[16,1088]{0,1:T(32,128)(4,1)S(1)}, pred[16,1088]{0,1:T(32,128)(4,1)}, u32[]{:S(2)}) copy-start(pred[16,1088]{0,1:T(32,128)(4,1)} %constant.152) | copy-start | bytes 52228
  264.6 210.4 %all-to-all-start.1 = ((bf16[128,16,256]{2,1,0:T(8,128)(2,1)}), bf16[128,16,256]{2,1,0:T(8,128)(2,1)}, u32[]{:S(2)}, u32[]{:S(2)}) async-start(bf16[128,16,256]{2,1,0:T(8,128)(2,1)} %bitcast.21), calls=%async_computation.1 | async-start | bytes 2097152 | tf_op jit(solution)/shard_map/all_to_all | solution.py:83
  410.3 7.4 %copy-start.4 = (bf16[256,256]{0,1:T(8,128)(2,1)S(1)}, bf16[256,256]{0,1:T(8,128)(2,1)}, u32[]{:S(2)}) copy-start(bf16[256,256]{0,1:T(8,128)(2,1)} %slice.147) | copy-start | bytes 393220
  410.3 8.0 %copy-start.5 = (bf16[16,799,1]{0,2,1:T(2,128)(2,1)S(1)}, bf16[16,799,1]{0,2,1:T(2,128)(2,1)}, u32[]{:S(2)}) copy-start(bf16[16,799,1]{0,2,1:T(2,128)(2,1)} %copy.28) | copy-start | bytes 76708
  410.3 8.0 %copy-start.18 = (pred[16,544]{0,1:T(32,128)(4,1)S(1)}, pred[16,544]{0,1:T(32,128)(4,1)}, u32[]{:S(2)}) copy-start(pred[16,544]{0,1:T(32,128)(4,1)} %constant.153) | copy-start | bytes 26116
  449.6 3.7 copy-start.9
  449.6 4.0 copy-start.10
  449.6 4.0 copy-start.19
  462.7 1.8 copy-start.11
  462.8 1.8 copy-start.20
  470.6 4.5 copy-start.14
  475.0 6.0 %copy-start.1 = (f32[512,256]{1,0:T(8,128)S(1)}, f32[512,256]{1,0:T(8,128)}, u32[]{:S(2)}) copy-start(f32[512,256]{1,0:T(8,128)} %param.10) | copy-start | bytes 1572868
  (6 other events, 9.5 us)
Sparse Core Ops, SparseCore 0:
  76.3 106.3 all-reduce.2
where the time goes:
time: 496 us; the launch traced here: 488 us
  matrix products  179 us (36%)
  waiting for transfers between devices  105 us (21%)
  other arithmetic  76.5 us (15%)
  local copies, waits for them, and re-layouts  75.8 us (15%)
  starting transfers between devices  35.3 us (7%)
  between operations  16.3 us (3%)
    conv_general_dilated x5, matrix products, filter_level(): lax.conv_general_dilated(joined[:, :, None], tap_rows[::-1][:, None, :],...  166 us
    psum x1, waiting for transfers between devices, local(): gram_total = lax.psum(partial_gram, 'grp')  105 us
    another operation x6, other arithmetic, basis_from(): lower_factor = jnp.linalg.cholesky(inner_gram)  34.4 us
    another operation x3, other arithmetic, basis_from(): jax.scipy.linalg.solve_triangular(lower_factor, product.T, lower=True)  19.7 us
    convert_element_type x6, local copies, waits for them, and re-layouts, local(): filtered.append(result_level.astype(jnp.bfloat16)[None])  15.2 us
    broadcast_in_dim x5, local copies, waits for them, and re-layouts, local(): filtered.append(result_level.astype(jnp.bfloat16)[None])  15.2 us
    ppermute x5, starting transfers between devices, shifted(): return lax.ppermute(x, axis, pairs)  14.9 us
    slice x4, local copies, waits for them, and re-layouts, filter_level(): tap_rows = basis_bf[::stride]  12.8 us
  transfers between devices with their start and end apart: 8, of which 2 were waited for; matrix products, arithmetic and copies ran while one was open for 47% of the time, Pallas kernels for 0%

commit v1 on v0

--- a/solution.py
+++ b/solution.py
@@ -76,7 +76,7 @@
     partial_gram = lax.dot_general(
         received, received, (((0,), (0,)), ((), ())), preferred_element_type=jnp.float32
     )
-    gram_total = lax.psum(partial_gram, "grp")
+    gram_total = jnp.sum(lax.all_gather(partial_gram, "grp"), axis=0)
     product = jnp.dot(gram_total, sketch, precision=highest)
     basis_bf, diag_here = basis_from(product)
     coeffs = jnp.dot(received, basis_bf, preferred_element_type=jnp.float32).astype(jnp.bfloat16)

time: 496 us -> 501 us (1.010)
  blocking collectives: 0 us -> 41.7 us
  waiting for transfers between devices: 105 us -> 77.4 us
  starting transfers between devices: 35.3 us -> 20.3 us
  other arithmetic: 76.5 us -> 91.2 us
    psum x1 -> x0, waiting for transfers between devices: 105 us -> none  [local(): gram_total = lax.psum(partial_gram, 'grp')]
    all_gather x0 -> x1, waiting for transfers between devices: none -> 65.6 us  [local(): gram_total = jnp.sum(lax.all_gather(partial_gram, 'grp'), axis=0)]
    all_to_all x0 -> x1, blocking collectives: none -> 41.7 us  [local(): lax.all_to_all(outgoing, ('bin', 'grp'), split_axis=0, concat_axis=0, til...]
    reduce_sum x0 -> x1, other arithmetic: none -> 12.3 us  [local(): gram_total = jnp.sum(lax.all_gather(partial_gram, 'grp'), axis=0)]
    all_to_all x1 -> x0, starting transfers between devices: 12 us -> none  [local(): lax.all_to_all(outgoing, ('bin', 'grp'), split_axis=0, concat_axis=0, til...]
    all_to_all x1, waiting for transfers between devices: 0.01 us -> 11.8 us  [local(): lax.all_to_all(coeffs, ('bin', 'grp'), split_axis=0, concat_axis=0, tiled...]
    mul x3, other arithmetic: 4.24 us -> 9.64 us  [strain_levels(): current = (paired[:, :, 0] + paired[:, :, 1]) * inv_root_two]
  transfers between devices with their start and end apart: 8 -> 7, of which waited for: 2 -> 2; matrix products, arithmetic and copies ran while one was open for 47% -> 8% of each run, Pallas kernels for 0% -> 0%
where the time goes in v1:
time: 501 us; the launch traced here: 496 us
  matrix products  174 us (35%)
  other arithmetic  91.2 us (18%)
  waiting for transfers between devices  77.4 us (15%)
  local copies, waits for them, and re-layouts  75.8 us (15%)
  blocking collectives  41.7 us (8%)
  starting transfers between devices  20.3 us (4%)
  between operations  16.4 us (3%)
    conv_general_dilated x5, matrix products, filter_level(): lax.conv_general_dilated(joined[:, :, None], tap_rows[::-1][:, None, :],...  166 us
    all_gather x1, waiting for transfers between devices, local(): gram_total = jnp.sum(lax.all_gather(partial_gram, 'grp'), axis=0)  65.6 us
    all_to_all x1, blocking collectives, local(): lax.all_to_all(outgoing, ('bin', 'grp'), split_axis=0, concat_axis=0, til...  41.7 us
    another operation x6, other arithmetic, basis_from(): lower_factor = jnp.linalg.cholesky(inner_gram)  34 us
    another operation x3, other arithmetic, basis_from(): jax.scipy.linalg.solve_triangular(lower_factor, product.T, lower=True)  20.4 us
    convert_element_type x6, local copies, waits for them, and re-layouts, local(): filtered.append(result_level.astype(jnp.bfloat16)[None])  15.4 us
    broadcast_in_dim x5, local copies, waits for them, and re-layouts, local(): filtered.append(result_level.astype(jnp.bfloat16)[None])  15.3 us
    ppermute x5, starting transfers between devices, shifted(): return lax.ppermute(x, axis, pairs)  13.2 us
  transfers between devices with their start and end apart: 7, of which 2 were waited for; matrix products, arithmetic and copies ran while one was open for 8% of the time, Pallas kernels for 0%

profile of v1, /device:TPU:1, one launch (start us, length us, event | category | flops | bytes accessed | tf_op | source)
XLA Modules:
  0.0 496.3 jit_solution(10699770187401592794)
XLA Ops:
  9.0 6.9 %scatter_custom_fusion = bf16[2048,512]{1,0:T(8,128)(2,1)S(1)} fusion(s32[1024]{0:T(1024)S(1)} %bitcast.148, bf16[1024,512]{1,0:T(8,128)(2,1)} %param.6, f32[512]{0:T(512)S(1)} %bitcast.154, f32[512]{0:T(512)S(1)} %bitcast.155, f32[512]{0:T(512)S(1)} %bitcast.152, f32[512]{0:T(512)S(1)} %bitcast.153, f32[]{:T(128)} %constant.105.clone.1, ...), kind=kCustom, calls=%fused_computation.26 | custom fusion | flops 6291456 | bytes 3161094 | tf_op jit(solution)/shard_map/scatter | solution.py:74
  15.9 41.7 %all_to_all.24 = bf16[128,16,512]{2,1,0:T(8,128)(2,1)S(1)} all-to-all(bf16[128,16,512]{2,1,0:T(8,128)(2,1)S(1)} %bitcast.136), channel_id=1, replica_groups=mesh['bin'=4,'grp'=32] {'bin','grp'}, dimensions={0} | all-to-all | bytes 4194304 | tf_op jit(solution)/shard_map/all_to_all | solution.py:75
  61.3 6.4 %reshape.114 = f32[2,4096,2]{2,1,0:T(8,128)} reshape(f32[2,8192]{1,0:T(2,128)S(1)} %copy-done.14) | data formatting | bytes 131072 | tf_op jit(solution)/shard_map/reshape | solution.py:31
  67.7 6.2 %fusion.3 = f32[2,4096]{1,0:T(2,128)S(1)} fusion(f32[2,4096,2]{2,1,0:T(8,128)} %reshape.114), kind=kLoop, calls=%fused_computation.25 | loop fusion | flops 16384 | bytes 98304 | tf_op jit(solution)/shard_map/mul | solution.py:32
  82.5 3.2 collective-permute-start.4
  96.5 3.5 collective-permute-start
  106.1 65.6 %all-gather.3.cloned.1.call-done = f32[16384,512]{1,0:T(8,128)} async-done(((f32[512,512]{1,0:T(8,128)}), f32[16384,512]{1,0:T(8,128)}) %all-gather.3.cloned.1.call-update) | async-done | bytes 33554448 | tf_op jit(solution)/shard_map/all_gather | solution.py:79
  171.7 12.3 %reduce_sum.19 = f32[512,512]{1,0:T(8,128)S(1)} reduce(f32[32,512,512]{2,1,0:T(8,128)} %bitcast.131, f32[]{:T(128)} %constant.105.clone.1), dimensions={0}, to_apply=%region_4.5 | reduce | flops 8126464 | bytes 34603012 | tf_op jit(solution)/shard_map/reduce_sum | solution.py:79
  186.2 11.7 %cholesky.50 = f32[128,128]{1,0:T(8,128)S(1)} custom-call(f32[128,128]{1,0:T(8,128)S(1)} %cholesky.118), custom_call_target="Cholesky" | custom-call | tf_op jit(solution)/shard_map/jit(cholesky)/cholesky | solution.py:52
  198.0 9.8 %custom-call.15 = f32[1,128,128]{1,2,0:T(8,128)S(1)} custom-call(f32[1,128,128]{2,1,0:T(8,128)S(1)} %get-tuple-element.30), custom_call_target="InvertDiagBlocksLowerTriangular" | custom-call | tf_op jit(solution)/shard_map/jit(cholesky)/cholesky | solution.py:52
  208.3 11.8 %cholesky.105 = f32[128,128]{1,0:T(8,128)S(1)} custom-call(f32[128,128]{1,0:T(8,128)S(1)} %convolution_subtract_fusion.1), custom_call_target="Cholesky" | custom-call | tf_op jit(solution)/shard_map/jit(cholesky)/cholesky | solution.py:52
  222.8 4.0 while.1
  226.9 19.7 %custom-call.16 = f32[2,128,128]{1,2,0:T(8,128)S(1)} custom-call(f32[2,128,128]{2,1,0:T(8,128)S(1)} %get-tuple-element.14), custom_call_target="InvertDiagBlocksLowerTriangular" | custom-call | tf_op jit(solution)/shard_map/jit(_solve_triangular)/triangular_solve | solution.py:53
  253.1 6.1 %slice.147 = bf16[256,256]{0,1:T(8,128)(2,1)S(1)} slice(bf16[512,256]{0,1:T(8,128)(2,1)S(1)} %fusion.31), slice={[0:512:2], [0:256:1]} | slice | bytes 262144 | tf_op jit(solution)/shard_map/slice | solution.py:38
  268.9 8.6 %select_convert_fusion.2 = bf16[16,272,256]{2,0,1:T(8,128)(2,1)S(1)} fusion(pred[16,272]{0,1:T(8,128)(4,1)S(1)} %copy-done.21, bf16[16,399,1]{0,2,1:T(2,128)(2,1)S(1)} %copy.56, bf16[128,1,256]{2,1,0:T(2,128)(2,1)S(1)} %copy.57), kind=kOutput, calls=%fused_computation.8 | convolution fusion | flops 287440896 | bytes 2310880 | tf_op jit(solution)/shard_map/conv_general_dilated | solution.py:40
  280.3 31.3 %select_convert_fusion.1 = bf16[16,544,256]{2,0,1:T(8,128)(2,1)S(1)} fusion(pred[16,544]{0,1:T(8,128)(4,1)S(1)} %bitcast.158, bf16[16,799,1]{0,2,1:T(2,128)(2,1)S(1)} %copy.53, bf16[256,1,256]{2,1,0:T(2,128)(2,1)S(1)} %copy.54), kind=kOutput, calls=%fused_computation.6 | convolution fusion | flops 1145307136 | bytes 4621792 | tf_op jit(solution)/shard_map/conv_general_dilated | solution.py:40
  311.6 3.8 copy.55
  315.9 122.7 %select_convert_fusion = bf16[16,1088,256]{2,0,1:T(8,128)(2,1)} fusion(pred[16,1088]{0,1:T(8,128)(4,1)S(1)} %bitcast.157, bf16[16,1599,1]{0,2,1:T(2,128)(2,1)S(1)} %copy-done.9, bf16[512,1,256]{2,1,0:T(2,128)(2,1)S(1)} %copy.51), kind=kOutput, calls=%fused_computation.5 | convolution fusion | flops 4572315648 | bytes 9243616 | tf_op jit(solution)/shard_map/conv_general_dilated | solution.py:40
  438.6 10.2 %copy.52 = bf16[16,1088,256]{2,1,0:T(8,128)(2,1)} copy(bf16[16,1088,256]{2,0,1:T(8,128)(2,1)} %select_convert_fusion) | data formatting | bytes 17825792 | tf_op jit(solution)/shard_map/convert_element_type | solution.py:96
  448.8 7.5 %slice_bitcast_fusion = bf16[1,2,8192,256]{3,2,1,0:T(8,128)(2,1)} fusion(bf16[2,8704,256]{2,1,0:T(8,128)(2,1)} %bitcast.130), kind=kLoop, calls=%fused_computation.7 | loop fusion | bytes 16777216 | tf_op jit(solution)/shard_map/broadcast_in_dim | solution.py:96
  458.0 7.1 %all-to-all-start.1 = ((bf16[128,16,256]{2,1,0:T(8,128)(2,1)}), bf16[128,16,256]{2,1,0:T(8,128)(2,1)S(1)}, u32[]{:S(2)}, u32[]{:S(2)}) async-start(bf16[128,16,256]{2,1,0:T(8,128)(2,1)} %bitcast.22), calls=%async_computation.1 | async-start | bytes 2097152 | tf_op jit(solution)/shard_map/all_to_all | solution.py:83
  468.0 4.5 slice_bitcast_fusion.1
  472.5 11.8 %all-to-all-done.1 = bf16[128,16,256]{2,1,0:T(8,128)(2,1)S(1)} async-done(((bf16[128,16,256]{2,1,0:T(8,128)(2,1)}), bf16[128,16,256]{2,1,0:T(8,128)(2,1)S(1)}, u32[]{:S(2)}, u32[]{:S(2)}) %all-to-all-start.1) | async-done | bytes 1048608 | tf_op jit(solution)/shard_map/all_to_all | solution.py:83
  484.2 5.0 %gather_fusion = bf16[1024,256]{1,0:T(8,128)(2,1)} fusion(bf16[2048,256]{1,0:T(8,128)(2,1)S(1)} %bitcast.132, s32[1024]{0:T(1024)S(1)} %copy-done.16), kind=kCustom, calls=%fused_computation | custom fusion | bytes 1052672 | tf_op jit(solution)/shard_map/gather | solution.py:84
  (173 shorter events, 62.6 us)
Async XLA Ops:
  7.2 176.8 %copy-start = (f32[512,256]{1,0:T(8,128)S(1)}, f32[512,256]{1,0:T(8,128)}, u32[]{:S(2)}) copy-start(f32[512,256]{1,0:T(8,128)} %param.10) | copy-start | bytes 1572868
  7.2 164.5 %all-gather.3.cloned.1.call-start = ((), (), s32[]{:S(2)}) async-start(), calls=%async_computation.2 | async-start | bytes 34603008 | tf_op jit(solution)/shard_map/all_gather | solution.py:79
  59.0 2.3 copy-start.14
  82.0 3.7 copy-start.3
  82.5 18.8 %collective-permute-start.4 = (bf16[2,32]{1,0:T(2,128)(2,1)S(1)}, bf16[2,32]{1,0:T(2,128)(2,1)S(1)}, u32[]{:S(2)}, u32[]{:S(2)}) collective-permute-start(bf16[2,32]{1,0:T(2,128)(2,1)S(1)} %slice.212), channel_id=1, source_target_pairs={{0,1},{1,2},{2,3},{3,4},{4,5},{5,6},{6,7},{7,8},{8,9},{9,10},{10,1... | collective-permute-start | bytes 392 | tf_op jit(solution)/shard_map/ppermute | solution.py:14
  86.4 5.7 %copy-start.2 = (f32[2,4096,2]{2,1,0:T(8,128)S(1)}, f32[2,4096,2]{2,1,0:T(8,128)}, u32[]{:S(2)}) copy-start(f32[2,4096,2]{2,1,0:T(8,128)} %reshape.114) | copy-start | bytes 196612
  86.4 15.3 %collective-permute-start.3 = (bf16[2,64]{1,0:T(2,128)(2,1)S(1)}, bf16[2,64]{1,0:T(2,128)(2,1)S(1)}, u32[]{:S(2)}, u32[]{:S(2)}) collective-permute-start(bf16[2,64]{1,0:T(2,128)(2,1)S(1)} %slice.207), channel_id=1, source_target_pairs={{0,1},{1,2},{2,3},{3,4},{4,5},{5,6},{6,7},{7,8},{8,9},{9,10},{10,1... | collective-permute-start | bytes 776 | tf_op jit(solution)/shard_map/ppermute | solution.py:14
  89.8 12.4 %collective-permute-start.2 = (bf16[2,128]{1,0:T(2,128)(2,1)S(1)}, bf16[2,128]{1,0:T(2,128)(2,1)S(1)}, u32[]{:S(2)}, u32[]{:S(2)}) collective-permute-start(bf16[2,128]{1,0:T(2,128)(2,1)S(1)} %slice.202), channel_id=1, source_target_pairs={{0,1},{1,2},{2,3},{3,4},{4,5},{5,6},{6,7},{7,8},{8,9},{9,10},{10,1... | collective-permute-start | bytes 1544 | tf_op jit(solution)/shard_map/ppermute | solution.py:14
  94.5 8.2 %collective-permute-start.1 = (bf16[2,256]{1,0:T(2,128)(2,1)S(1)}, bf16[2,256]{1,0:T(2,128)(2,1)S(1)}, u32[]{:S(2)}, u32[]{:S(2)}) collective-permute-start(bf16[2,256]{1,0:T(2,128)(2,1)S(1)} %slice.196), channel_id=1, source_target_pairs={{0,1},{1,2},{2,3},{3,4},{4,5},{5,6},{6,7},{7,8},{8,9},{9,10},{10,1... | collective-permute-start | bytes 3080 | tf_op jit(solution)/shard_map/ppermute | solution.py:14
  96.5 7.3 %collective-permute-start = (bf16[2,512]{1,0:T(2,128)(2,1)S(1)}, bf16[2,512]{1,0:T(2,128)(2,1)S(1)}, u32[]{:S(2)}, u32[]{:S(2)}) collective-permute-start(bf16[2,512]{1,0:T(2,128)(2,1)S(1)} %slice.190), channel_id=1, source_target_pairs={{0,1},{1,2},{2,3},{3,4},{4,5},{5,6},{6,7},{7,8},{8,9},{9,10},{10,1... | collective-permute-start | bytes 6152 | tf_op jit(solution)/shard_map/ppermute | solution.py:14
  226.8 35.6 %copy-start.23 = (pred[16,68]{0,1:T(8,128)(4,1)S(1)}, pred[16,68]{0,1:T(8,128)(4,1)}, u32[]{:S(2)}) copy-start(pred[16,68]{0,1:T(8,128)(4,1)} %constant.156) | copy-start | bytes 3268
  267.1 1.8 copy-start.21
  278.2 2.1 copy-start.20
  311.6 3.8 copy-start.8
  311.6 4.2 copy-start.9
  311.6 4.2 copy-start.19
  448.8 7.5 %copy-start.7 = (bf16[128,16,512]{2,1,0:T(8,128)(2,1)S(1)}, bf16[128,16,512]{2,1,0:T(8,128)(2,1)}, u32[]{:S(2)}) copy-start(bf16[128,16,512]{2,1,0:T(8,128)(2,1)} %copy-done.6) | copy-start | bytes 6291460
  448.8 7.5 %copy-start.11 = (bf16[128,512]{1,0:T(8,128)(2,1)S(1)}, bf16[128,512]{1,0:T(8,128)(2,1)}, u32[]{:S(2)}) copy-start(bf16[128,512]{1,0:T(8,128)(2,1)} %copy-done.10) | copy-start | bytes 393220
  448.8 7.5 %copy-start.13 = (bf16[128,512]{1,0:T(8,128)(2,1)S(1)}, bf16[128,512]{1,0:T(8,128)(2,1)}, u32[]{:S(2)}) copy-start(bf16[128,512]{1,0:T(8,128)(2,1)} %copy-done.12) | copy-start | bytes 393220
  458.0 7.1 %copy-start.4 = (s32[256,1]{0,1:T(1,128)S(1)}, s32[256,1]{0,1:T(1,128)}, u32[]{:S(2)}) copy-start(s32[256,1]{0,1:T(1,128)} %shift-left_or_fusion) | copy-start | bytes 3076
  458.0 7.1 %copy-start.5 = (f32[256,256]{1,0:T(8,128)S(1)}, f32[256,256]{1,0:T(8,128)}, u32[]{:S(2)}) copy-start(f32[256,256]{1,0:T(8,128)} %get-tuple-element.24) | copy-start | bytes 786436
  458.0 26.2 %all-to-all-start.1 = ((bf16[128,16,256]{2,1,0:T(8,128)(2,1)}), bf16[128,16,256]{2,1,0:T(8,128)(2,1)S(1)}, u32[]{:S(2)}, u32[]{:S(2)}) async-start(bf16[128,16,256]{2,1,0:T(8,128)(2,1)} %bitcast.22), calls=%async_computation.1 | async-start | bytes 2097152 | tf_op jit(solution)/shard_map/all_to_all | solution.py:83
  468.0 16.2 %copy-start.16 = (s32[1024]{0:T(1024)S(1)}, s32[1024]{0:T(1024)}, u32[]{:S(2)}) copy-start(s32[1024]{0:T(1024)} %broadcast_clamp_fusion) | copy-start | bytes 12292
  484.2 5.0 %copy-start.1 = (f32[512,256]{1,0:T(8,128)S(1)}, f32[512,256]{1,0:T(8,128)}, u32[]{:S(2)}) copy-start(f32[512,256]{1,0:T(8,128)} %param.10) | copy-start | bytes 1572868
  (7 other events, 9.2 us)
Sparse Core Ops, SparseCore 0:
  61.4 110.2 all-gather.2
